TPU v7x, 32 devices: a whole 2x2x4 slice. The times are simulated.
32 devices in a mesh: space: 4 (over y, core), vel: 8 (over z, x).
Axes of the slice: x: 2, y: 2, z: 4, core: 2. Of those that a mesh axis runs over, the one named last changes fastest.
Arguments:
- distribution: float32 [64, 48, 2304], P('space', 'vel'), may hold values from 0 to 2
- collision_rate: float32 [64], P('space'), may hold values from 0.1 to 1
- face_flags: int32 [64], replicated, may hold values 0 or 1
Outputs:
- updated: float32 [64, 48, 2304], P('space', 'vel')
All inputs are finite; a program needn't handle non-finite values.
Results may differ from a plain program's by a relative error of at most 0.0001.
Values sent between devices are 32-bit elements; how exact they have to be, the bound alone decides.
A program may use at most 64 MiB of HBM per device.

v0:
```python
import math
import jax
import jax.numpy as jnp
from jax import lax
from jax.sharding import PartitionSpec as P

NV = 48
LENGTH = 8.0
RADIUS = 6.0
COURANT = 0.9
GOLDEN = (1.0 + math.sqrt(5.0)) / 2.0
DIRECTIONS = (
    (0.0, 1.0, GOLDEN),
    (0.0, -1.0, GOLDEN),
    (1.0, GOLDEN, 0.0),
    (-1.0, GOLDEN, 0.0),
    (GOLDEN, 0.0, 1.0),
    (-GOLDEN, 0.0, 1.0),
)
HIGHEST_MODE = lax.Precision.HIGHEST


def padded_2(cells, sides, width):
    for axis, dim in sides:
        count = lax.axis_size(axis)
        ends = count - 1
        head = lax.slice_in_dim(cells, 0, width, axis=dim)
        tail = lax.slice_in_dim(cells, cells.shape[dim] - width, cells.shape[dim], axis=dim)
        cells = jnp.concatenate(
            [
                lax.ppermute(tail, axis, [(i, (i + 1) % count) for i in range(ends)]),
                cells,
                lax.ppermute(head, axis, [((i + 1) % count, i) for i in range(ends)]),
            ],
            axis=dim,
        )
    return cells


def kernel_tables(points):
    index = jnp.arange(points, dtype=jnp.int32)
    wrapped = jnp.where(
        index < points // 2, index, jnp.where(index == points // 2, 0, index - points)
    )
    signed = wrapped.astype(jnp.float32) * (math.pi / LENGTH)
    wave_x = signed[:, None, None]
    wave_y = signed[None, :, None]
    wave_z = signed[None, None, :]
    square = wave_x * wave_x + wave_y * wave_y + wave_z * wave_z
    scale = math.sqrt(1.0 + GOLDEN * GOLDEN)
    gain_tables = []
    loss_tables = []
    for direction in DIRECTIONS:
        parallel = (wave_x * direction[0] + wave_y * direction[1] + wave_z * direction[2]) / scale
        across = jnp.sqrt(jnp.maximum(square - parallel * parallel, 0.0))
        gain_tables.append(jnp.cos(0.5 * RADIUS * parallel))
        loss_tables.append(jnp.sinc(RADIUS * across / (2.0 * math.pi)))
    loss_total = sum(loss_tables) / 6.0
    return (gain_tables, loss_tables, loss_total)


def dft_tables(points):
    index = jnp.arange(points, dtype=jnp.int32)
    product = index[:, None] * index[None, :] % points
    angle = product.astype(jnp.float32) * (2.0 * math.pi / points)
    cosine = jnp.cos(angle)
    sine = jnp.sin(angle)
    first_table = jnp.stack([cosine, -sine], axis=1)
    forward_table = jnp.stack(
        [jnp.stack([cosine, -sine], axis=1), jnp.stack([sine, cosine], axis=1)], axis=1
    )
    inverse_table = jnp.stack(
        [jnp.stack([cosine, sine], axis=1), jnp.stack([-sine, cosine], axis=1)], axis=1
    )
    return (first_table, forward_table, inverse_table)


def apply_table(tensor, table, dims):
    return lax.dot_general(
        tensor,
        table,
        ((dims, tuple(range(len(dims)))), ((), ())),
        precision=HIGHEST_MODE,
        preferred_element_type=jnp.float32,
    )


def forward_cube(cube, tables):
    first_table, forward_table, inverse_table = tables
    section_one = apply_table(cube, first_table, (1,))
    section_two = apply_table(section_one, forward_table, (1, 2))
    return apply_table(section_two, forward_table, (0, 2))


def inverse_pair(spectrum, tables):
    first_table, forward_table, inverse_table = tables
    points = spectrum.shape[0]
    section_one = apply_table(spectrum, inverse_table, (3, 2))
    section_two = apply_table(section_one, inverse_table, (0, 2))
    section_three = apply_table(section_two, inverse_table, (0, 2))
    section_three = section_three * (1.0 / float(points**3))
    return (section_three[:, :, 0, :], section_three[:, :, 1, :])


def packed(spectrum, first_factor, second_factor):
    real_part = spectrum[:, :, 0, :]
    imag_part = spectrum[:, :, 1, :]
    first_factor = jnp.asarray(first_factor, jnp.float32)
    first_factor = first_factor[:, :, :] if first_factor.ndim == 3 else first_factor
    joined_real = first_factor * real_part - second_factor * imag_part
    joined_imag = first_factor * imag_part + second_factor * real_part
    return jnp.stack([joined_real, joined_imag], axis=2)


def collide(spectrum, kernels, tables):
    gain_tables, loss_tables, loss_total = kernels
    products = []
    for gain_table, loss_table in zip(gain_tables, loss_tables):
        first_part, second_part = inverse_pair(packed(spectrum, gain_table, loss_table), tables)
        products.append(first_part * second_part)
    gain_total = sum(products) / 6.0
    cube, loss_field = inverse_pair(packed(spectrum, 1.0, loss_total), tables)
    return gain_total - cube * loss_field


def body(distribution, collision_rate, face_flags):
    cell_count, planes_dev, width = distribution.shape
    points = NV
    tables = dft_tables(points)
    kernels = kernel_tables(points)

    def from_cell(one_cell):
        cube = one_cell.reshape(points, points, points)
        spectrum = forward_cube(cube, tables)
        return collide(spectrum, kernels, tables).reshape(points, width)

    regrouped = lax.all_to_all(distribution, "vel", split_axis=0, concat_axis=1, tiled=True)
    cell_terms = lax.map(from_cell, regrouped)
    collision_term = lax.all_to_all(cell_terms, "vel", split_axis=1, concat_axis=0, tiled=True)
    offset = lax.axis_index("space") * cell_count
    padded = padded_2(distribution, (("space", 0),), 1)
    mirror = distribution.reshape(cell_count, planes_dev, points, points)[:, :, ::-1, :].reshape(
        cell_count, planes_dev, width
    )
    wall_flags = jnp.concatenate([face_flags, jnp.ones((1,), jnp.int32)])
    nearby_walls = lax.dynamic_slice_in_dim(wall_flags, offset, cell_count + 1)
    lower_wall = (nearby_walls[:-1] == 1)[:, None, None]
    upper_wall = (nearby_walls[1:] == 1)[:, None, None]
    at_start = (offset + jnp.arange(cell_count, dtype=jnp.int32) == 0)[:, None, None]
    lower_side = jnp.where(lower_wall, mirror, jnp.where(at_start, distribution, padded[:-2]))
    upper_side = jnp.where(upper_wall, mirror, padded[2:])
    column = (jnp.arange(width, dtype=jnp.int32) // points).astype(jnp.float32)
    centre = (points - 1) / 2.0
    speed = COURANT * (column - centre) / centre
    upwind_flux = jnp.where(
        speed > 0, speed * (distribution - lower_side), speed * (upper_side - distribution)
    )
    return distribution - upwind_flux + collision_rate[:, None, None] * collision_term


def solution(mesh):
    return jax.shard_map(
        body,
        mesh=mesh,
        in_specs=(P("space", "vel", None), P("space"), P()),
        out_specs=P("space", "vel", None),
        check_vma=False,
    )
```

profile of v0, /device:TPU:0, one launch (start us, length us, event | category | flops | bytes accessed | tf_op | source)
XLA Modules:
  0.0 418.8 jit_solution(5220611589307567298)
XLA Ops:
  2.8 7.3 %all-to-all-start = ((f32[16,6,2304]{2,1,0:T(8,128)}), f32[16,6,2304]{2,1,0:T(8,128)S(1)}, u32[]{:S(2)}, u32[]{:S(2)}) async-start(f32[16,6,2304]{2,1,0:T(8,128)} %copy.77), calls=%async_computation | async-start | bytes 2359296 | tf_op jit(solution)/shard_map/all_to_all | solution.py:137
  10.6 13.5 %add_multiply_fusion = (f32[48,48,48]{2,1,0:T(8,128)}, f32[48,48,48]{2,1,0:T(8,128)}, f32[48,48,48]{2,1,0:T(8,128)}, f32[48,48,48]{2,1,0:T(8,128)}, f32[48,48,48...) fusion(f32[48]{0:T(128)S(1)} %get-tuple-element.737, f32[48,48]{1,0:T(8,128)S(1)} %get-tuple-element.739, ...), kind=kLoop, calls=%fused_computation.329 | loop fusion | flops 26652672 | bytes 3161856 | tf_op jit(solution)/shard_map/div | solution.py:58
  24.2 14.4 %all-to-all-done = f32[16,6,2304]{2,1,0:T(8,128)S(1)} async-done(((f32[16,6,2304]{2,1,0:T(8,128)}), f32[16,6,2304]{2,1,0:T(8,128)S(1)}, u32[]{:S(2)}, u32[]{:S(2)}) %all-to-all-start) | async-done | bytes 884768 | tf_op jit(solution)/shard_map/all_to_all | solution.py:137
  39.3 347.2 %while.13 = (s32[]{:T(128)}, f32[2,48,2304]{2,0,1:T(2,128)}, f32[2,48,2304]{2,0,1:T(2,128)S(1)}, f32[48,2,48]{2,0,1:T(8,128)S(1)}, f32[48,2,2,48]{3,0,1,2:T(8,12...) while((s32[]{:T(128)}, f32[2,48,2304]{2,0,1:T(2,128)}, ...), condition=%wide.region_1.3_spmd.clone.clone.clone, body=%wide.region_0.2_spmd.clone.clone.clone.sunk | while | flops 5998288896 | bytes 128030208 | solution.py:138
  45.1 3.9 copy.170
  49.0 6.0 %fusion.365 = f32[48,48,2,48,1]{0,3,4,2,1:T(8,128)S(1)} fusion(f32[48,48,2,48,1]{1,0,2,4,3:T(8,128)} %copy.170, f32[48,2,2,48]{3,0,1,2:T(8,128)S(1)} %get-tuple-element.770), kind=kOutput, calls=%fused_computation.156.clone.1 | convolution fusion | flops 254803968 | bytes 1806336 | tf_op jit(solution)/shard_map/while/body/eval_jaxpr/dot_general | solution.py:79
  57.1 10.0 %fusion.367 = (f32[48,48,1,48]{3,1,2,0:T(8,128)}, f32[48,48,1,48]{3,1,2,0:T(8,128)}, f32[48,48,1,48]{3,1,2,0:T(8,128)S(1)}, f32[48,48,1,48]{3,1,2,0:T(8,128)S(1)...) fusion(f32[48,48,48]{2,1,0:T(8,128)S(1)} %copy-done.16, f32[48]{0:T(128)S(1)} %get-tuple-element.779, ...), kind=kLoop, calls=%fused_computation.117.clone.1 | loop fusion | flops 2211840 | bytes 4884672 | tf_op jit(solution)/shard_map/while/body/eval_jaxpr/sub | solution.py:110
  67.1 3.5 fusion.380
  70.6 3.9 copy.176
  74.5 6.0 %fusion.381 = f32[48,48,2,48,1]{0,3,4,2,1:T(8,128)S(1)} fusion(f32[48,48,2,48,1]{0,1,2,4,3:T(8,128)} %copy.176, f32[48,2,2,48]{3,0,1,2:T(8,128)S(1)} %get-tuple-element.772), kind=kOutput, calls=%fused_computation.148.clone.1 | convolution fusion | flops 254803968 | bytes 1806336 | tf_op jit(solution)/shard_map/while/body/eval_jaxpr/dot_general | solution.py:79
  80.5 3.5 bitcast_multiply_fusion.45
  84.0 3.5 fusion.382
  87.5 3.9 copy.177
  91.4 6.0 %fusion.383 = f32[48,48,2,48,1]{0,3,4,2,1:T(8,128)S(1)} fusion(f32[48,48,2,48,1]{0,1,2,4,3:T(8,128)} %copy.177, f32[48,2,2,48]{3,0,1,2:T(8,128)S(1)} %get-tuple-element.772), kind=kOutput, calls=%fused_computation.152.clone.1 | convolution fusion | flops 254803968 | bytes 1806336 | tf_op jit(solution)/shard_map/while/body/eval_jaxpr/dot_general | solution.py:79
  97.4 3.5 bitcast_multiply_fusion.46
  101.0 9.6 %fusion.370 = (f32[48,48,1,48]{3,1,2,0:T(8,128)}, f32[48,48,1,48]{3,1,2,0:T(8,128)}, f32[48,48,1,48]{3,1,2,0:T(8,128)S(1)}, f32[48,48,1,48]{3,1,2,0:T(8,128)S(1)}) fusion(f32[48,48,48]{2,1,0:T(8,128)S(1)} %copy-done.18, f32[48]{0:T(128)S(1)} %get-tuple-element.785, f32[48,48]{1,0:T(8,128)S(1)} %copy-done.24, f32[48,48,2,48]{3,1,2,0:T(8,128)S(1)} %fusion.366, ...), kind=kLoop, calls=%fused_computation.93.clone.1 | loop fusion | flops 1769472 | bytes 3557568 | tf_op jit(solution)/shard_map/while/body/eval_jaxpr/sub | solution.py:110
  114.0 4.0 copy.172
  118.0 6.0 %fusion.372 = f32[48,48,2,48,1]{0,3,4,2,1:T(8,128)S(1)} fusion(f32[48,48,2,48,1]{0,1,2,4,3:T(8,128)} %copy.172, f32[48,2,2,48]{3,0,1,2:T(8,128)S(1)} %get-tuple-element.772), kind=kOutput, calls=%fused_computation.132.clone.1 | convolution fusion | flops 254803968 | bytes 1806336 | tf_op jit(solution)/shard_map/while/body/eval_jaxpr/dot_general | solution.py:79
  127.5 3.5 fusion.373
  131.0 4.1 copy.173
  135.2 6.0 %fusion.374 = f32[48,48,2,48,1]{0,3,4,2,1:T(8,128)S(1)} fusion(f32[48,48,2,48,1]{0,1,2,4,3:T(8,128)} %copy.173, f32[48,2,2,48]{3,0,1,2:T(8,128)S(1)} %get-tuple-element.772), kind=kOutput, calls=%fused_computation.136.clone.1 | convolution fusion | flops 254803968 | bytes 1806336 | tf_op jit(solution)/shard_map/while/body/eval_jaxpr/dot_general | solution.py:79
  141.2 3.5 bitcast_multiply_fusion.42
  144.8 9.6 %fusion.375 = (f32[48,48,1,48]{3,1,2,0:T(8,128)}, f32[48,48,1,48]{3,1,2,0:T(8,128)}, f32[48,48,1,48]{3,1,2,0:T(8,128)S(1)}, f32[48,48,1,48]{3,1,2,0:T(8,128)S(1)}) fusion(f32[48,48,48]{2,1,0:T(8,128)S(1)} %copy-done.14, f32[48]{0:T(128)S(1)} %get-tuple-element.782, f32[48,48]{1,0:T(8,128)S(1)} %copy-done.26, f32[48,48,2,48]{3,1,2,0:T(8,128)S(1)} %fusion.366, ...), kind=kLoop, calls=%fused_computation.105.clone.1 | loop fusion | flops 1769472 | bytes 3557568 | tf_op jit(solution)/shard_map/while/body/eval_jaxpr/sub | solution.py:110
  159.2 6.0 %fusion.377 = f32[48,48,2,48,1]{0,3,4,2,1:T(8,128)S(1)} fusion(f32[48,48,2,48,1]{0,1,2,4,3:T(8,128)} %copy.174, f32[48,2,2,48]{3,0,1,2:T(8,128)S(1)} %get-tuple-element.772), kind=kOutput, calls=%fused_computation.140.clone.1 | convolution fusion | flops 254803968 | bytes 1806336 | tf_op jit(solution)/shard_map/while/body/eval_jaxpr/dot_general | solution.py:79
  167.3 3.5 fusion.378
  170.8 3.9 copy.175
  174.7 6.0 %fusion.379 = f32[48,48,2,48,1]{0,3,4,2,1:T(8,128)S(1)} fusion(f32[48,48,2,48,1]{0,1,2,4,3:T(8,128)} %copy.175, f32[48,2,2,48]{3,0,1,2:T(8,128)S(1)} %get-tuple-element.772), kind=kOutput, calls=%fused_computation.144.clone.1 | convolution fusion | flops 254803968 | bytes 1806336 | tf_op jit(solution)/shard_map/while/body/eval_jaxpr/dot_general | solution.py:79
  180.8 3.5 bitcast_multiply_fusion.44
  184.2 3.5 fusion.368
  187.7 3.9 copy.171
  191.7 6.2 %fusion.369 = f32[48,48,2,48,1]{0,3,4,2,1:T(8,128)S(1)} fusion(f32[48,48,2,48,1]{0,1,2,4,3:T(8,128)} %copy.171, f32[48,2,2,48]{3,0,1,2:T(8,128)S(1)} %get-tuple-element.772), kind=kOutput, calls=%fused_computation.128.clone.1 | convolution fusion | flops 254803968 | bytes 1806336 | tf_op jit(solution)/shard_map/while/body/eval_jaxpr/dot_general | solution.py:79
  200.2 4.2 fusion.384
  216.8 3.6 copy.170
  220.4 6.0 %fusion.365 = f32[48,48,2,48,1]{0,3,4,2,1:T(8,128)S(1)} fusion(f32[48,48,2,48,1]{1,0,2,4,3:T(8,128)} %copy.170, f32[48,2,2,48]{3,0,1,2:T(8,128)S(1)} %get-tuple-element.770), kind=kOutput, calls=%fused_computation.156.clone.1 | convolution fusion | flops 254803968 | bytes 1806336 | tf_op jit(solution)/shard_map/while/body/eval_jaxpr/dot_general | solution.py:79
  228.6 10.0 %fusion.367 = (f32[48,48,1,48]{3,1,2,0:T(8,128)}, f32[48,48,1,48]{3,1,2,0:T(8,128)}, f32[48,48,1,48]{3,1,2,0:T(8,128)S(1)}, f32[48,48,1,48]{3,1,2,0:T(8,128)S(1)...) fusion(f32[48,48,48]{2,1,0:T(8,128)S(1)} %copy-done.16, f32[48]{0:T(128)S(1)} %get-tuple-element.779, ...), kind=kLoop, calls=%fused_computation.117.clone.1 | loop fusion | flops 2211840 | bytes 4884672 | tf_op jit(solution)/shard_map/while/body/eval_jaxpr/sub | solution.py:110
  238.5 3.5 fusion.380
  242.0 3.9 copy.176
  246.0 6.0 %fusion.381 = f32[48,48,2,48,1]{0,3,4,2,1:T(8,128)S(1)} fusion(f32[48,48,2,48,1]{0,1,2,4,3:T(8,128)} %copy.176, f32[48,2,2,48]{3,0,1,2:T(8,128)S(1)} %get-tuple-element.772), kind=kOutput, calls=%fused_computation.148.clone.1 | convolution fusion | flops 254803968 | bytes 1806336 | tf_op jit(solution)/shard_map/while/body/eval_jaxpr/dot_general | solution.py:79
  252.0 3.5 bitcast_multiply_fusion.45
  255.5 3.5 fusion.382
  259.0 3.9 copy.177
  262.9 6.0 %fusion.383 = f32[48,48,2,48,1]{0,3,4,2,1:T(8,128)S(1)} fusion(f32[48,48,2,48,1]{0,1,2,4,3:T(8,128)} %copy.177, f32[48,2,2,48]{3,0,1,2:T(8,128)S(1)} %get-tuple-element.772), kind=kOutput, calls=%fused_computation.152.clone.1 | convolution fusion | flops 254803968 | bytes 1806336 | tf_op jit(solution)/shard_map/while/body/eval_jaxpr/dot_general | solution.py:79
  269.0 3.5 bitcast_multiply_fusion.46
  272.5 9.6 %fusion.370 = (f32[48,48,1,48]{3,1,2,0:T(8,128)}, f32[48,48,1,48]{3,1,2,0:T(8,128)}, f32[48,48,1,48]{3,1,2,0:T(8,128)S(1)}, f32[48,48,1,48]{3,1,2,0:T(8,128)S(1)}) fusion(f32[48,48,48]{2,1,0:T(8,128)S(1)} %copy-done.18, f32[48]{0:T(128)S(1)} %get-tuple-element.785, f32[48,48]{1,0:T(8,128)S(1)} %copy-done.24, f32[48,48,2,48]{3,1,2,0:T(8,128)S(1)} %fusion.366, ...), kind=kLoop, calls=%fused_computation.93.clone.1 | loop fusion | flops 1769472 | bytes 3557568 | tf_op jit(solution)/shard_map/while/body/eval_jaxpr/sub | solution.py:110
  285.5 4.2 %copy.172 = f32[48,48,2,48,1]{0,1,2,4,3:T(8,128)} copy(f32[48,48,2,48,1]{3,1,2,0,4:T(8,128)} %fusion.371) | data formatting | bytes 1769472 | tf_op jit(solution)/shard_map/while/body/eval_jaxpr/dot_general | solution.py:79
  289.8 6.0 %fusion.372 = f32[48,48,2,48,1]{0,3,4,2,1:T(8,128)S(1)} fusion(f32[48,48,2,48,1]{0,1,2,4,3:T(8,128)} %copy.172, f32[48,2,2,48]{3,0,1,2:T(8,128)S(1)} %get-tuple-element.772), kind=kOutput, calls=%fused_computation.132.clone.1 | convolution fusion | flops 254803968 | bytes 1806336 | tf_op jit(solution)/shard_map/while/body/eval_jaxpr/dot_general | solution.py:79
  295.8 3.5 bitcast_multiply_fusion.41
  299.3 3.5 fusion.373
  302.8 3.8 copy.173
  306.6 6.0 %fusion.374 = f32[48,48,2,48,1]{0,3,4,2,1:T(8,128)S(1)} fusion(f32[48,48,2,48,1]{0,1,2,4,3:T(8,128)} %copy.173, f32[48,2,2,48]{3,0,1,2:T(8,128)S(1)} %get-tuple-element.772), kind=kOutput, calls=%fused_computation.136.clone.1 | convolution fusion | flops 254803968 | bytes 1806336 | tf_op jit(solution)/shard_map/while/body/eval_jaxpr/dot_general | solution.py:79
  312.7 3.5 bitcast_multiply_fusion.42
  316.3 9.6 %fusion.375 = (f32[48,48,1,48]{3,1,2,0:T(8,128)}, f32[48,48,1,48]{3,1,2,0:T(8,128)}, f32[48,48,1,48]{3,1,2,0:T(8,128)S(1)}, f32[48,48,1,48]{3,1,2,0:T(8,128)S(1)}) fusion(f32[48,48,48]{2,1,0:T(8,128)S(1)} %copy-done.14, f32[48]{0:T(128)S(1)} %get-tuple-element.782, f32[48,48]{1,0:T(8,128)S(1)} %copy-done.26, f32[48,48,2,48]{3,1,2,0:T(8,128)S(1)} %fusion.366, ...), kind=kLoop, calls=%fused_computation.105.clone.1 | loop fusion | flops 1769472 | bytes 3557568 | tf_op jit(solution)/shard_map/while/body/eval_jaxpr/sub | solution.py:110
  330.7 6.0 %fusion.377 = f32[48,48,2,48,1]{0,3,4,2,1:T(8,128)S(1)} fusion(f32[48,48,2,48,1]{0,1,2,4,3:T(8,128)} %copy.174, f32[48,2,2,48]{3,0,1,2:T(8,128)S(1)} %get-tuple-element.772), kind=kOutput, calls=%fused_computation.140.clone.1 | convolution fusion | flops 254803968 | bytes 1806336 | tf_op jit(solution)/shard_map/while/body/eval_jaxpr/dot_general | solution.py:79
  338.8 3.5 fusion.378
  342.3 4.0 copy.175
  346.3 6.0 %fusion.379 = f32[48,48,2,48,1]{0,3,4,2,1:T(8,128)S(1)} fusion(f32[48,48,2,48,1]{0,1,2,4,3:T(8,128)} %copy.175, f32[48,2,2,48]{3,0,1,2:T(8,128)S(1)} %get-tuple-element.772), kind=kOutput, calls=%fused_computation.144.clone.1 | convolution fusion | flops 254803968 | bytes 1806336 | tf_op jit(solution)/shard_map/while/body/eval_jaxpr/dot_general | solution.py:79
  352.3 3.5 bitcast_multiply_fusion.44
  355.8 3.5 fusion.368
  359.3 4.0 copy.171
  363.3 6.2 %fusion.369 = f32[48,48,2,48,1]{0,3,4,2,1:T(8,128)S(1)} fusion(f32[48,48,2,48,1]{0,1,2,4,3:T(8,128)} %copy.171, f32[48,2,2,48]{3,0,1,2:T(8,128)S(1)} %get-tuple-element.772), kind=kOutput, calls=%fused_computation.128.clone.1 | convolution fusion | flops 254803968 | bytes 1806336 | tf_op jit(solution)/shard_map/while/body/eval_jaxpr/dot_general | solution.py:79
  371.8 4.2 fusion.384
  386.5 4.4 %all-to-all-start.1 = ((f32[2,48,2304]{2,0,1:T(2,128)}), f32[2,48,2304]{2,0,1:T(2,128)}, u32[]{:S(2)}, u32[]{:S(2)}) async-start(f32[2,48,2304]{2,0,1:T(2,128)} %get-tuple-element.142), calls=%async_computation.1 | async-start | bytes 1769472 | tf_op jit(solution)/shard_map/all_to_all | solution.py:139
  396.8 3.5 rev.3
  402.2 10.9 %all-to-all-done.1 = f32[2,48,2304]{2,0,1:T(2,128)} async-done(((f32[2,48,2304]{2,0,1:T(2,128)}), f32[2,48,2304]{2,0,1:T(2,128)}, u32[]{:S(2)}, u32[]{:S(2)}) %all-to-all-start.1) | async-done | bytes 884768 | tf_op jit(solution)/shard_map/all_to_all | solution.py:139
  (174 shorter events, 74.0 us)
Async XLA Ops:
  2.8 35.8 %all-to-all-start = ((f32[16,6,2304]{2,1,0:T(8,128)}), f32[16,6,2304]{2,1,0:T(8,128)S(1)}, u32[]{:S(2)}, u32[]{:S(2)}) async-start(f32[16,6,2304]{2,1,0:T(8,128)} %copy.77), calls=%async_computation | async-start | bytes 2359296 | tf_op jit(solution)/shard_map/all_to_all | solution.py:137
  10.0 14.1 %copy-start.31 = (f32[48]{0:T(128)}, f32[48]{0:T(128)S(1)}, u32[]{:S(2)}) copy-start(f32[48]{0:T(128)S(1)} %get-tuple-element.734) | copy-start | bytes 580
  10.6 13.6 %copy-start.21 = (f32[48,48]{1,0:T(8,128)}, f32[48,48]{1,0:T(8,128)S(1)}, u32[]{:S(2)}) copy-start(f32[48,48]{1,0:T(8,128)S(1)} %get-tuple-element.736) | copy-start | bytes 27652
  10.6 13.6 %copy-start.23 = (f32[48,48]{1,0:T(8,128)}, f32[48,48]{1,0:T(8,128)S(1)}, u32[]{:S(2)}) copy-start(f32[48,48]{1,0:T(8,128)S(1)} %get-tuple-element.738) | copy-start | bytes 27652
  10.6 13.6 %copy-start.25 = (f32[48,48]{1,0:T(8,128)}, f32[48,48]{1,0:T(8,128)S(1)}, u32[]{:S(2)}) copy-start(f32[48,48]{1,0:T(8,128)S(1)} %get-tuple-element.735) | copy-start | bytes 27652
  10.6 13.6 %copy-start.27 = (f32[48,48]{1,0:T(8,128)}, f32[48,48]{1,0:T(8,128)S(1)}, u32[]{:S(2)}) copy-start(f32[48,48]{1,0:T(8,128)S(1)} %get-tuple-element.732) | copy-start | bytes 27652
  38.6 0.7 copy-start.32
  55.0 2.1 copy-start.12
  55.0 2.1 copy-start.15
  55.0 2.1 copy-start.16
  55.0 2.1 copy-start.28
  80.5 3.5 copy-start.6
  80.5 3.5 copy-start.7
  97.4 3.6 copy-start.17
  97.4 3.5 copy-start.18
  97.4 3.5 copy-start.24
  124.0 3.5 copy-start.10
  124.0 3.5 copy-start.11
  141.2 3.6 copy-start.13
  141.2 3.6 copy-start.14
  141.2 3.6 copy-start.22
  141.2 3.6 copy-start.26
  165.2 2.1 copy-start.8
  165.2 2.1 copy-start.9
  180.7 3.5 copy-start.4
  180.8 3.5 copy-start.5
  191.7 8.3 %copy-start.2 = (f32[48,48,2,48]{3,1,2,0:T(8,128)S(1)}, f32[48,48,2,48]{3,1,2,0:T(8,128)}, u32[]{:S(2)}) copy-start(f32[48,48,2,48]{3,1,2,0:T(8,128)} %bitcast_multiply_fusion.41) | copy-start | bytes 2654212 | tf_op jit(solution)/shard_map/while
  191.7 8.3 %copy-start.3 = (f32[48,48,2,48]{3,1,2,0:T(8,128)S(1)}, f32[48,48,2,48]{3,1,2,0:T(8,128)}, u32[]{:S(2)}) copy-start(f32[48,48,2,48]{3,1,2,0:T(8,128)} %bitcast_multiply_fusion.42) | copy-start | bytes 2654212 | tf_op jit(solution)/shard_map/while
  197.9 2.1 copy-start
  197.9 2.4 copy-start.1
  204.4 2.4 copy-start.29
  209.8 1.0 copy-start.30
  226.4 2.1 copy-start.12
  226.4 2.1 copy-start.15
  226.5 2.1 copy-start.16
  226.5 2.1 copy-start.28
  252.0 3.5 copy-start.6
  252.0 3.5 copy-start.7
  268.9 3.6 copy-start.17
  269.0 3.5 copy-start.18
  269.0 3.5 copy-start.24
  295.8 3.5 copy-start.10
  295.8 3.5 copy-start.11
  312.7 3.6 copy-start.13
  312.7 3.6 copy-start.14
  312.7 3.6 copy-start.22
  312.7 3.6 copy-start.26
  336.7 2.1 copy-start.8
  336.8 2.1 copy-start.9
  352.3 3.5 copy-start.4
  352.3 3.5 copy-start.5
  363.3 8.3 %copy-start.2 = (f32[48,48,2,48]{3,1,2,0:T(8,128)S(1)}, f32[48,48,2,48]{3,1,2,0:T(8,128)}, u32[]{:S(2)}) copy-start(f32[48,48,2,48]{3,1,2,0:T(8,128)} %bitcast_multiply_fusion.41) | copy-start | bytes 2654212 | tf_op jit(solution)/shard_map/while
  363.3 8.3 %copy-start.3 = (f32[48,48,2,48]{3,1,2,0:T(8,128)S(1)}, f32[48,48,2,48]{3,1,2,0:T(8,128)}, u32[]{:S(2)}) copy-start(f32[48,48,2,48]{3,1,2,0:T(8,128)} %bitcast_multiply_fusion.42) | copy-start | bytes 2654212 | tf_op jit(solution)/shard_map/while
  369.5 2.1 copy-start
  369.5 2.4 copy-start.1
  376.0 2.4 copy-start.29
  381.4 1.0 copy-start.30
  386.5 4.4 %copy-start.19 = (f32[16,6,2304]{2,0,1:T(8,128)S(1)}, f32[16,6,2304]{2,0,1:T(8,128)}, u32[]{:S(2)}) copy-start(f32[16,6,2304]{2,0,1:T(8,128)} %param.6) | copy-start | bytes 2654212
  386.5 7.1 %copy-start.34 = (s32[64]{0:T(128)S(1)}, s32[64]{0:T(128)}, u32[]{:S(2)}) copy-start(s32[64]{0:T(128)} %param.8) | copy-start | bytes 772
  386.5 26.5 %all-to-all-start.1 = ((f32[2,48,2304]{2,0,1:T(2,128)}), f32[2,48,2304]{2,0,1:T(2,128)}, u32[]{:S(2)}, u32[]{:S(2)}) async-start(f32[2,48,2304]{2,0,1:T(2,128)} %get-tuple-element.142), calls=%async_computation.1 | async-start | bytes 1769472 | tf_op jit(solution)/shard_map/all_to_all | solution.py:139
  391.0 26.1 %collective-permute-start = (f32[1,6,2304]{2,0,1:T(1,128)S(1)}, f32[1,6,2304]{2,0,1:T(1,128)S(1)}, u32[]{:S(2)}, u32[]{:S(2)}) collective-permute-start(f32[1,6,2304]{2,0,1:T(1,128)S(1)} %get-tuple-element.523), channel_id=1, source_target_pairs={{0,8},{8,16},{16,24},{1,9},{9,17},{17,25},{2,10},{10,18},{18,26},{... | collective-permute-start | bytes 165896 | tf_op jit(solution)/shard_map/ppermute | solution.py:31
  392.3 24.9 %collective-permute-start.1 = (f32[1,6,2304]{2,0,1:T(1,128)S(1)}, f32[1,6,2304]{2,0,1:T(1,128)S(1)}, u32[]{:S(2)}, u32[]{:S(2)}) collective-permute-start(f32[1,6,2304]{2,0,1:T(1,128)S(1)} %get-tuple-element.524), channel_id=1, source_target_pairs={{8,0},{16,8},{24,16},{9,1},{17,9},{25,17},{10,2},{18,10},{26,18},{... | collective-permute-start | bytes 165896 | tf_op jit(solution)/shard_map/ppermute | solution.py:33
  415.3 1.9 copy-start.20
  415.3 1.9 copy-start.33
where the time goes:
time: 423 us; the launch traced here: 419 us
  matrix products  196 us (46%)
  local copies, waits for them, and re-layouts  94.4 us (22%)
  other arithmetic  82.4 us (19%)
  waiting for transfers between devices  25.3 us (6%)
  starting transfers between devices  14.2 us (3%)
  loops' own time  5.61 us (1%)
    dot_general x48, matrix products, apply_table(): lax.dot_general(tensor, table, ((dims, tuple(range(len(dims)))), ((), ())...  196 us
    dot_general x16, local copies, waits for them, and re-layouts, apply_table(): lax.dot_general(tensor, table, ((dims, tuple(range(len(dims)))), ((), ())...  60.6 us
    sub x6, other arithmetic, packed(): joined_real = first_factor * real_part - second_factor * imag_part  58.4 us
    all_to_all x1, waiting for transfers between devices, body(): lax.all_to_all(distribution, 'vel', split_axis=0, concat_axis=1, tiled=True)  14.4 us
    div x1, other arithmetic, kernel_tables(): loss_total = sum(loss_tables) / 6.0  13.5 us
    all_to_all x1, waiting for transfers between devices, body(): lax.all_to_all(cell_terms, 'vel', split_axis=1, concat_axis=0, tiled=True)  10.9 us
  transfers between devices with their start and end apart: 4, of which 2 were waited for; matrix products, arithmetic and copies ran while one was open for 6% of the time, Pallas kernels for 0%

commit v1 on v0

--- a/solution.py
+++ b/solution.py
@@ -136,7 +136,10 @@
 
     regrouped = lax.all_to_all(distribution, "vel", split_axis=0, concat_axis=1, tiled=True)
     cell_terms = lax.map(from_cell, regrouped)
-    collision_term = lax.all_to_all(cell_terms, "vel", split_axis=1, concat_axis=0, tiled=True)
+    collision_term = jnp.concatenate(
+        lax.all_to_all(jnp.stack(jnp.split(cell_terms, lax.axis_size("vel"), axis=1)), "vel", 0, 0),
+        axis=0,
+    )
     offset = lax.axis_index("space") * cell_count
     padded = padded_2(distribution, (("space", 0),), 1)
     mirror = distribution.reshape(cell_count, planes_dev, points, points)[:, :, ::-1, :].reshape(

time: 423 us -> 435 us (1.028)
  local copies, waits for them, and re-layouts: 94.4 us -> 107 us
    unnamed x22 -> x29, local copies, waits for them, and re-layouts: 3.04 us -> 14 us
where the time goes in v1:
time: 435 us; the launch traced here: 431 us
  matrix products  196 us (45%)
  local copies, waits for them, and re-layouts  107 us (25%)
  other arithmetic  82.4 us (19%)
  waiting for transfers between devices  25.3 us (6%)
  starting transfers between devices  14.1 us (3%)
  loops' own time  5.72 us (1%)
    dot_general x48, matrix products, apply_table(): lax.dot_general(tensor, table, ((dims, tuple(range(len(dims)))), ((), ())...  196 us
    dot_general x16, local copies, waits for them, and re-layouts, apply_table(): lax.dot_general(tensor, table, ((dims, tuple(range(len(dims)))), ((), ())...  60.6 us
    sub x6, other arithmetic, packed(): joined_real = first_factor * real_part - second_factor * imag_part  58.4 us
    all_to_all x1, waiting for transfers between devices, body(): lax.all_to_all(distribution, 'vel', split_axis=0, concat_axis=1, tiled=True)  14.4 us
    unnamed x29, local copies, waits for them, and re-layouts  14 us
    div x1, other arithmetic, kernel_tables(): loss_total = sum(loss_tables) / 6.0  13.5 us
    all_to_all x1, waiting for transfers between devices, body(): lax.all_to_all(jnp.stack(jnp.split(cell_terms, lax.axis_size('vel'), axis...  10.9 us
  transfers between devices with their start and end apart: 4, of which 2 were waited for; matrix products, arithmetic and copies ran while one was open for 6% of the time, Pallas kernels for 0%

profile of v1, /device:TPU:0, one launch (start us, length us, event | category | flops | bytes accessed | tf_op | source)
XLA Modules:
  0.0 431.1 jit_solution(18243857552264541438)
XLA Ops:
  2.8 7.3 %all-to-all-start = ((f32[16,6,2304]{2,1,0:T(8,128)}), f32[16,6,2304]{2,1,0:T(8,128)S(1)}, u32[]{:S(2)}, u32[]{:S(2)}) async-start(f32[16,6,2304]{2,1,0:T(8,128)} %copy.61), calls=%async_computation | async-start | bytes 2359296 | tf_op jit(solution)/shard_map/all_to_all | solution.py:137
  10.6 13.5 %add_multiply_fusion = (f32[48,48,48]{2,1,0:T(8,128)}, f32[48,48,48]{2,1,0:T(8,128)}, f32[48,48,48]{2,1,0:T(8,128)}, f32[48,48,48]{2,1,0:T(8,128)}, f32[48,48,48...) fusion(f32[48]{0:T(128)S(1)} %get-tuple-element.715, f32[48,48]{1,0:T(8,128)S(1)} %get-tuple-element.717, ...), kind=kLoop, calls=%fused_computation.329 | loop fusion | flops 26652672 | bytes 3161856 | tf_op jit(solution)/shard_map/div | solution.py:58
  24.2 14.4 %all-to-all-done = f32[16,6,2304]{2,1,0:T(8,128)S(1)} async-done(((f32[16,6,2304]{2,1,0:T(8,128)}), f32[16,6,2304]{2,1,0:T(8,128)S(1)}, u32[]{:S(2)}, u32[]{:S(2)}) %all-to-all-start) | async-done | bytes 884768 | tf_op jit(solution)/shard_map/all_to_all | solution.py:137
  39.3 347.1 %while.13 = (s32[]{:T(128)}, f32[2,48,2304]{2,0,1:T(2,128)}, f32[2,48,2304]{2,0,1:T(2,128)S(1)}, f32[48,2,48]{2,0,1:T(8,128)S(1)}, f32[48,2,2,48]{3,0,1,2:T(8,12...) while((s32[]{:T(128)}, f32[2,48,2304]{2,0,1:T(2,128)}, ...), condition=%wide.region_1.3_spmd.clone.clone.clone, body=%wide.region_0.2_spmd.clone.clone.clone.sunk | while | flops 5998288896 | bytes 128030208 | solution.py:138
  45.1 3.9 copy.161
  49.0 6.0 %fusion.365 = f32[48,48,2,48,1]{0,3,4,2,1:T(8,128)S(1)} fusion(f32[48,48,2,48,1]{1,0,2,4,3:T(8,128)} %copy.161, f32[48,2,2,48]{3,0,1,2:T(8,128)S(1)} %get-tuple-element.748), kind=kOutput, calls=%fused_computation.156.clone.1 | convolution fusion | flops 254803968 | bytes 1806336 | tf_op jit(solution)/shard_map/while/body/eval_jaxpr/dot_general | solution.py:79
  57.1 10.0 %fusion.367 = (f32[48,48,1,48]{3,1,2,0:T(8,128)}, f32[48,48,1,48]{3,1,2,0:T(8,128)}, f32[48,48,1,48]{3,1,2,0:T(8,128)S(1)}, f32[48,48,1,48]{3,1,2,0:T(8,128)S(1)...) fusion(f32[48,48,48]{2,1,0:T(8,128)S(1)} %copy-done.16, f32[48]{0:T(128)S(1)} %get-tuple-element.757, ...), kind=kLoop, calls=%fused_computation.117.clone.1 | loop fusion | flops 2211840 | bytes 4884672 | tf_op jit(solution)/shard_map/while/body/eval_jaxpr/sub | solution.py:110
  67.1 3.5 fusion.380
  70.6 3.9 copy.167
  74.5 6.0 %fusion.381 = f32[48,48,2,48,1]{0,3,4,2,1:T(8,128)S(1)} fusion(f32[48,48,2,48,1]{0,1,2,4,3:T(8,128)} %copy.167, f32[48,2,2,48]{3,0,1,2:T(8,128)S(1)} %get-tuple-element.750), kind=kOutput, calls=%fused_computation.148.clone.1 | convolution fusion | flops 254803968 | bytes 1806336 | tf_op jit(solution)/shard_map/while/body/eval_jaxpr/dot_general | solution.py:79
  80.5 3.5 bitcast_multiply_fusion.45
  84.0 3.5 fusion.382
  87.5 3.9 copy.168
  91.4 6.0 %fusion.383 = f32[48,48,2,48,1]{0,3,4,2,1:T(8,128)S(1)} fusion(f32[48,48,2,48,1]{0,1,2,4,3:T(8,128)} %copy.168, f32[48,2,2,48]{3,0,1,2:T(8,128)S(1)} %get-tuple-element.750), kind=kOutput, calls=%fused_computation.152.clone.1 | convolution fusion | flops 254803968 | bytes 1806336 | tf_op jit(solution)/shard_map/while/body/eval_jaxpr/dot_general | solution.py:79
  97.4 3.5 bitcast_multiply_fusion.46
  101.0 9.6 %fusion.370 = (f32[48,48,1,48]{3,1,2,0:T(8,128)}, f32[48,48,1,48]{3,1,2,0:T(8,128)}, f32[48,48,1,48]{3,1,2,0:T(8,128)S(1)}, f32[48,48,1,48]{3,1,2,0:T(8,128)S(1)}) fusion(f32[48,48,48]{2,1,0:T(8,128)S(1)} %copy-done.18, f32[48]{0:T(128)S(1)} %get-tuple-element.763, f32[48,48]{1,0:T(8,128)S(1)} %copy-done.24, f32[48,48,2,48]{3,1,2,0:T(8,128)S(1)} %fusion.366, ...), kind=kLoop, calls=%fused_computation.93.clone.1 | loop fusion | flops 1769472 | bytes 3557568 | tf_op jit(solution)/shard_map/while/body/eval_jaxpr/sub | solution.py:110
  114.0 4.0 copy.163
  118.0 6.0 %fusion.372 = f32[48,48,2,48,1]{0,3,4,2,1:T(8,128)S(1)} fusion(f32[48,48,2,48,1]{0,1,2,4,3:T(8,128)} %copy.163, f32[48,2,2,48]{3,0,1,2:T(8,128)S(1)} %get-tuple-element.750), kind=kOutput, calls=%fused_computation.132.clone.1 | convolution fusion | flops 254803968 | bytes 1806336 | tf_op jit(solution)/shard_map/while/body/eval_jaxpr/dot_general | solution.py:79
  124.0 3.5 bitcast_multiply_fusion.41
  127.5 3.5 fusion.373
  131.0 4.1 copy.164
  135.2 6.0 %fusion.374 = f32[48,48,2,48,1]{0,3,4,2,1:T(8,128)S(1)} fusion(f32[48,48,2,48,1]{0,1,2,4,3:T(8,128)} %copy.164, f32[48,2,2,48]{3,0,1,2:T(8,128)S(1)} %get-tuple-element.750), kind=kOutput, calls=%fused_computation.136.clone.1 | convolution fusion | flops 254803968 | bytes 1806336 | tf_op jit(solution)/shard_map/while/body/eval_jaxpr/dot_general | solution.py:79
  141.2 3.5 bitcast_multiply_fusion.42
  144.8 9.6 %fusion.375 = (f32[48,48,1,48]{3,1,2,0:T(8,128)}, f32[48,48,1,48]{3,1,2,0:T(8,128)}, f32[48,48,1,48]{3,1,2,0:T(8,128)S(1)}, f32[48,48,1,48]{3,1,2,0:T(8,128)S(1)}) fusion(f32[48,48,48]{2,1,0:T(8,128)S(1)} %copy-done.14, f32[48]{0:T(128)S(1)} %get-tuple-element.760, f32[48,48]{1,0:T(8,128)S(1)} %copy-done.26, f32[48,48,2,48]{3,1,2,0:T(8,128)S(1)} %fusion.366, ...), kind=kLoop, calls=%fused_computation.105.clone.1 | loop fusion | flops 1769472 | bytes 3557568 | tf_op jit(solution)/shard_map/while/body/eval_jaxpr/sub | solution.py:110
  159.2 6.0 %fusion.377 = f32[48,48,2,48,1]{0,3,4,2,1:T(8,128)S(1)} fusion(f32[48,48,2,48,1]{0,1,2,4,3:T(8,128)} %copy.165, f32[48,2,2,48]{3,0,1,2:T(8,128)S(1)} %get-tuple-element.750), kind=kOutput, calls=%fused_computation.140.clone.1 | convolution fusion | flops 254803968 | bytes 1806336 | tf_op jit(solution)/shard_map/while/body/eval_jaxpr/dot_general | solution.py:79
  167.3 3.5 fusion.378
  170.8 3.9 copy.166
  174.7 6.0 %fusion.379 = f32[48,48,2,48,1]{0,3,4,2,1:T(8,128)S(1)} fusion(f32[48,48,2,48,1]{0,1,2,4,3:T(8,128)} %copy.166, f32[48,2,2,48]{3,0,1,2:T(8,128)S(1)} %get-tuple-element.750), kind=kOutput, calls=%fused_computation.144.clone.1 | convolution fusion | flops 254803968 | bytes 1806336 | tf_op jit(solution)/shard_map/while/body/eval_jaxpr/dot_general | solution.py:79
  180.8 3.5 bitcast_multiply_fusion.44
  184.2 3.5 fusion.368
  187.7 3.9 copy.162
  191.7 6.2 %fusion.369 = f32[48,48,2,48,1]{0,3,4,2,1:T(8,128)S(1)} fusion(f32[48,48,2,48,1]{0,1,2,4,3:T(8,128)} %copy.162, f32[48,2,2,48]{3,0,1,2:T(8,128)S(1)} %get-tuple-element.750), kind=kOutput, calls=%fused_computation.128.clone.1 | convolution fusion | flops 254803968 | bytes 1806336 | tf_op jit(solution)/shard_map/while/body/eval_jaxpr/dot_general | solution.py:79
  200.2 4.2 fusion.384
  216.7 3.6 copy.161
  220.3 6.0 %fusion.365 = f32[48,48,2,48,1]{0,3,4,2,1:T(8,128)S(1)} fusion(f32[48,48,2,48,1]{1,0,2,4,3:T(8,128)} %copy.161, f32[48,2,2,48]{3,0,1,2:T(8,128)S(1)} %get-tuple-element.748), kind=kOutput, calls=%fused_computation.156.clone.1 | convolution fusion | flops 254803968 | bytes 1806336 | tf_op jit(solution)/shard_map/while/body/eval_jaxpr/dot_general | solution.py:79
  228.5 10.0 %fusion.367 = (f32[48,48,1,48]{3,1,2,0:T(8,128)}, f32[48,48,1,48]{3,1,2,0:T(8,128)}, f32[48,48,1,48]{3,1,2,0:T(8,128)S(1)}, f32[48,48,1,48]{3,1,2,0:T(8,128)S(1)...) fusion(f32[48,48,48]{2,1,0:T(8,128)S(1)} %copy-done.16, f32[48]{0:T(128)S(1)} %get-tuple-element.757, ...), kind=kLoop, calls=%fused_computation.117.clone.1 | loop fusion | flops 2211840 | bytes 4884672 | tf_op jit(solution)/shard_map/while/body/eval_jaxpr/sub | solution.py:110
  238.5 3.5 fusion.380
  241.9 3.9 copy.167
  245.9 6.0 %fusion.381 = f32[48,48,2,48,1]{0,3,4,2,1:T(8,128)S(1)} fusion(f32[48,48,2,48,1]{0,1,2,4,3:T(8,128)} %copy.167, f32[48,2,2,48]{3,0,1,2:T(8,128)S(1)} %get-tuple-element.750), kind=kOutput, calls=%fused_computation.148.clone.1 | convolution fusion | flops 254803968 | bytes 1806336 | tf_op jit(solution)/shard_map/while/body/eval_jaxpr/dot_general | solution.py:79
  251.9 3.5 bitcast_multiply_fusion.45
  255.4 3.5 fusion.382
  258.9 3.9 copy.168
  262.8 6.0 %fusion.383 = f32[48,48,2,48,1]{0,3,4,2,1:T(8,128)S(1)} fusion(f32[48,48,2,48,1]{0,1,2,4,3:T(8,128)} %copy.168, f32[48,2,2,48]{3,0,1,2:T(8,128)S(1)} %get-tuple-element.750), kind=kOutput, calls=%fused_computation.152.clone.1 | convolution fusion | flops 254803968 | bytes 1806336 | tf_op jit(solution)/shard_map/while/body/eval_jaxpr/dot_general | solution.py:79
  268.9 3.5 bitcast_multiply_fusion.46
  272.4 9.6 %fusion.370 = (f32[48,48,1,48]{3,1,2,0:T(8,128)}, f32[48,48,1,48]{3,1,2,0:T(8,128)}, f32[48,48,1,48]{3,1,2,0:T(8,128)S(1)}, f32[48,48,1,48]{3,1,2,0:T(8,128)S(1)}) fusion(f32[48,48,48]{2,1,0:T(8,128)S(1)} %copy-done.18, f32[48]{0:T(128)S(1)} %get-tuple-element.763, f32[48,48]{1,0:T(8,128)S(1)} %copy-done.24, f32[48,48,2,48]{3,1,2,0:T(8,128)S(1)} %fusion.366, ...), kind=kLoop, calls=%fused_computation.93.clone.1 | loop fusion | flops 1769472 | bytes 3557568 | tf_op jit(solution)/shard_map/while/body/eval_jaxpr/sub | solution.py:110
  285.5 4.2 copy.163
  289.7 6.0 %fusion.372 = f32[48,48,2,48,1]{0,3,4,2,1:T(8,128)S(1)} fusion(f32[48,48,2,48,1]{0,1,2,4,3:T(8,128)} %copy.163, f32[48,2,2,48]{3,0,1,2:T(8,128)S(1)} %get-tuple-element.750), kind=kOutput, calls=%fused_computation.132.clone.1 | convolution fusion | flops 254803968 | bytes 1806336 | tf_op jit(solution)/shard_map/while/body/eval_jaxpr/dot_general | solution.py:79
  299.2 3.5 fusion.373
  302.7 3.8 copy.164
  306.6 6.0 %fusion.374 = f32[48,48,2,48,1]{0,3,4,2,1:T(8,128)S(1)} fusion(f32[48,48,2,48,1]{0,1,2,4,3:T(8,128)} %copy.164, f32[48,2,2,48]{3,0,1,2:T(8,128)S(1)} %get-tuple-element.750), kind=kOutput, calls=%fused_computation.136.clone.1 | convolution fusion | flops 254803968 | bytes 1806336 | tf_op jit(solution)/shard_map/while/body/eval_jaxpr/dot_general | solution.py:79
  312.6 3.5 bitcast_multiply_fusion.42
  316.2 9.6 %fusion.375 = (f32[48,48,1,48]{3,1,2,0:T(8,128)}, f32[48,48,1,48]{3,1,2,0:T(8,128)}, f32[48,48,1,48]{3,1,2,0:T(8,128)S(1)}, f32[48,48,1,48]{3,1,2,0:T(8,128)S(1)}) fusion(f32[48,48,48]{2,1,0:T(8,128)S(1)} %copy-done.14, f32[48]{0:T(128)S(1)} %get-tuple-element.760, f32[48,48]{1,0:T(8,128)S(1)} %copy-done.26, f32[48,48,2,48]{3,1,2,0:T(8,128)S(1)} %fusion.366, ...), kind=kLoop, calls=%fused_computation.105.clone.1 | loop fusion | flops 1769472 | bytes 3557568 | tf_op jit(solution)/shard_map/while/body/eval_jaxpr/sub | solution.py:110
  330.6 6.0 %fusion.377 = f32[48,48,2,48,1]{0,3,4,2,1:T(8,128)S(1)} fusion(f32[48,48,2,48,1]{0,1,2,4,3:T(8,128)} %copy.165, f32[48,2,2,48]{3,0,1,2:T(8,128)S(1)} %get-tuple-element.750), kind=kOutput, calls=%fused_computation.140.clone.1 | convolution fusion | flops 254803968 | bytes 1806336 | tf_op jit(solution)/shard_map/while/body/eval_jaxpr/dot_general | solution.py:79
  338.7 3.5 fusion.378
  342.2 4.0 copy.166
  346.2 6.0 %fusion.379 = f32[48,48,2,48,1]{0,3,4,2,1:T(8,128)S(1)} fusion(f32[48,48,2,48,1]{0,1,2,4,3:T(8,128)} %copy.166, f32[48,2,2,48]{3,0,1,2:T(8,128)S(1)} %get-tuple-element.750), kind=kOutput, calls=%fused_computation.144.clone.1 | convolution fusion | flops 254803968 | bytes 1806336 | tf_op jit(solution)/shard_map/while/body/eval_jaxpr/dot_general | solution.py:79
  352.2 3.5 bitcast_multiply_fusion.44
  355.7 3.5 fusion.368
  359.2 4.0 copy.162
  363.2 6.2 %fusion.369 = f32[48,48,2,48,1]{0,3,4,2,1:T(8,128)S(1)} fusion(f32[48,48,2,48,1]{0,1,2,4,3:T(8,128)} %copy.162, f32[48,2,2,48]{3,0,1,2:T(8,128)S(1)} %get-tuple-element.750), kind=kOutput, calls=%fused_computation.128.clone.1 | convolution fusion | flops 254803968 | bytes 1806336 | tf_op jit(solution)/shard_map/while/body/eval_jaxpr/dot_general | solution.py:79
  371.7 4.2 fusion.384
  398.9 4.2 all-to-all-start.1
  409.0 3.5 rev.3
  414.4 10.9 %all-to-all-done.1 = f32[8,2,6,2304]{3,1,2,0:T(2,128)} async-done(((f32[8,2,6,2304]{3,1,2,0:T(2,128)}), f32[8,2,6,2304]{3,1,2,0:T(2,128)}, u32[]{:S(2)}, u32[]{:S(2)}) %all-to-all-start.1) | async-done | bytes 884768 | tf_op jit(solution)/shard_map/all_to_all | solution.py:140
  (182 shorter events, 86.3 us)
Async XLA Ops:
  2.8 35.8 %all-to-all-start = ((f32[16,6,2304]{2,1,0:T(8,128)}), f32[16,6,2304]{2,1,0:T(8,128)S(1)}, u32[]{:S(2)}, u32[]{:S(2)}) async-start(f32[16,6,2304]{2,1,0:T(8,128)} %copy.61), calls=%async_computation | async-start | bytes 2359296 | tf_op jit(solution)/shard_map/all_to_all | solution.py:137
  10.0 14.1 %copy-start.31 = (f32[48]{0:T(128)}, f32[48]{0:T(128)S(1)}, u32[]{:S(2)}) copy-start(f32[48]{0:T(128)S(1)} %get-tuple-element.712) | copy-start | bytes 580
  10.6 13.6 %copy-start.21 = (f32[48,48]{1,0:T(8,128)}, f32[48,48]{1,0:T(8,128)S(1)}, u32[]{:S(2)}) copy-start(f32[48,48]{1,0:T(8,128)S(1)} %get-tuple-element.714) | copy-start | bytes 27652
  10.6 13.6 %copy-start.23 = (f32[48,48]{1,0:T(8,128)}, f32[48,48]{1,0:T(8,128)S(1)}, u32[]{:S(2)}) copy-start(f32[48,48]{1,0:T(8,128)S(1)} %get-tuple-element.716) | copy-start | bytes 27652
  10.6 13.6 %copy-start.25 = (f32[48,48]{1,0:T(8,128)}, f32[48,48]{1,0:T(8,128)S(1)}, u32[]{:S(2)}) copy-start(f32[48,48]{1,0:T(8,128)S(1)} %get-tuple-element.713) | copy-start | bytes 27652
  10.6 13.6 %copy-start.27 = (f32[48,48]{1,0:T(8,128)}, f32[48,48]{1,0:T(8,128)S(1)}, u32[]{:S(2)}) copy-start(f32[48,48]{1,0:T(8,128)S(1)} %get-tuple-element.710) | copy-start | bytes 27652
  38.6 0.7 copy-start.32
  55.0 2.1 copy-start.12
  55.0 2.1 copy-start.15
  55.0 2.1 copy-start.16
  55.0 2.1 copy-start.28
  80.5 3.5 copy-start.6
  80.5 3.5 copy-start.7
  97.4 3.6 copy-start.17
  97.4 3.5 copy-start.18
  97.4 3.5 copy-start.24
  124.0 3.5 copy-start.10
  124.0 3.5 copy-start.11
  141.2 3.6 copy-start.13
  141.2 3.6 copy-start.14
  141.2 3.6 copy-start.22
  141.2 3.6 copy-start.26
  165.2 2.1 copy-start.8
  165.2 2.1 copy-start.9
  180.7 3.5 copy-start.4
  180.8 3.5 copy-start.5
  191.7 8.3 %copy-start.2 = (f32[48,48,2,48]{3,1,2,0:T(8,128)S(1)}, f32[48,48,2,48]{3,1,2,0:T(8,128)}, u32[]{:S(2)}) copy-start(f32[48,48,2,48]{3,1,2,0:T(8,128)} %bitcast_multiply_fusion.41) | copy-start | bytes 2654212 | tf_op jit(solution)/shard_map/while
  191.7 8.3 %copy-start.3 = (f32[48,48,2,48]{3,1,2,0:T(8,128)S(1)}, f32[48,48,2,48]{3,1,2,0:T(8,128)}, u32[]{:S(2)}) copy-start(f32[48,48,2,48]{3,1,2,0:T(8,128)} %bitcast_multiply_fusion.42) | copy-start | bytes 2654212 | tf_op jit(solution)/shard_map/while
  197.9 2.1 copy-start
  197.9 2.4 copy-start.1
  204.4 2.4 copy-start.29
  209.8 0.9 copy-start.30
  226.3 2.1 copy-start.12
  226.4 2.1 copy-start.15
  226.4 2.1 copy-start.16
  226.4 2.1 copy-start.28
  251.9 3.5 copy-start.6
  251.9 3.5 copy-start.7
  268.9 3.6 copy-start.17
  268.9 3.5 copy-start.18
  268.9 3.5 copy-start.24
  295.7 3.5 copy-start.10
  295.7 3.5 copy-start.11
  312.6 3.6 copy-start.13
  312.6 3.6 copy-start.14
  312.6 3.6 copy-start.22
  312.6 3.6 copy-start.26
  336.6 2.1 copy-start.8
  336.7 2.1 copy-start.9
  352.2 3.5 copy-start.4
  352.2 3.5 copy-start.5
  363.2 8.3 %copy-start.2 = (f32[48,48,2,48]{3,1,2,0:T(8,128)S(1)}, f32[48,48,2,48]{3,1,2,0:T(8,128)}, u32[]{:S(2)}) copy-start(f32[48,48,2,48]{3,1,2,0:T(8,128)} %bitcast_multiply_fusion.41) | copy-start | bytes 2654212 | tf_op jit(solution)/shard_map/while
  363.2 8.3 %copy-start.3 = (f32[48,48,2,48]{3,1,2,0:T(8,128)S(1)}, f32[48,48,2,48]{3,1,2,0:T(8,128)}, u32[]{:S(2)}) copy-start(f32[48,48,2,48]{3,1,2,0:T(8,128)} %bitcast_multiply_fusion.42) | copy-start | bytes 2654212 | tf_op jit(solution)/shard_map/while
  369.4 2.1 copy-start
  369.4 2.4 copy-start.1
  375.9 2.4 copy-start.29
  381.3 0.9 copy-start.30
  394.2 9.0 %copy-start.19 = (f32[16,6,2304]{2,0,1:T(8,128)S(1)}, f32[16,6,2304]{2,0,1:T(8,128)}, u32[]{:S(2)}) copy-start(f32[16,6,2304]{2,0,1:T(8,128)} %param.6) | copy-start | bytes 2654212
  395.8 10.0 %copy-start.34 = (s32[64]{0:T(128)S(1)}, s32[64]{0:T(128)}, u32[]{:S(2)}) copy-start(s32[64]{0:T(128)} %param.8) | copy-start | bytes 772
  398.9 26.4 %all-to-all-start.1 = ((f32[8,2,6,2304]{3,1,2,0:T(2,128)}), f32[8,2,6,2304]{3,1,2,0:T(2,128)}, u32[]{:S(2)}, u32[]{:S(2)}) async-start(f32[8,2,6,2304]{3,1,2,0:T(2,128)} %bitcast_dynamic-update-slice_fusion), calls=%async_computation.1 | async-start | bytes 1769472 | tf_op jit(solution)/shard_map/all_to_all | solution.py:140
  403.3 26.1 %collective-permute-start = (f32[1,6,2304]{2,0,1:T(1,128)S(1)}, f32[1,6,2304]{2,0,1:T(1,128)S(1)}, u32[]{:S(2)}, u32[]{:S(2)}) collective-permute-start(f32[1,6,2304]{2,0,1:T(1,128)S(1)} %get-tuple-element.501), channel_id=1, source_target_pairs={{0,8},{8,16},{16,24},{1,9},{9,17},{17,25},{2,10},{10,18},{18,26},{... | collective-permute-start | bytes 165896 | tf_op jit(solution)/shard_map/ppermute | solution.py:31
  404.6 24.9 %collective-permute-start.1 = (f32[1,6,2304]{2,0,1:T(1,128)S(1)}, f32[1,6,2304]{2,0,1:T(1,128)S(1)}, u32[]{:S(2)}, u32[]{:S(2)}) collective-permute-start(f32[1,6,2304]{2,0,1:T(1,128)S(1)} %get-tuple-element.502), channel_id=1, source_target_pairs={{8,0},{16,8},{24,16},{9,1},{17,9},{25,17},{10,2},{18,10},{26,18},{... | collective-permute-start | bytes 165896 | tf_op jit(solution)/shard_map/ppermute | solution.py:33
  427.5 1.9 copy-start.20
  427.5 1.9 copy-start.33
